TPU v7x, 128 devices: a whole 4x4x4 slice. The times are simulated.
128 devices in a mesh: grp: 8 (over y, core), dom: 16 (over z, x).
Axes of the slice: x: 4, y: 4, z: 4, core: 2. Of those that a mesh axis runs over, the one named last changes fastest.
Arguments:
- diag_blocks: bfloat16 [2048, 384, 384], P(('grp', 'dom')), may hold values from -0.3125 to 0.3125
- face_in: bfloat16 [4096, 384, 384], P(('grp', 'dom')), may hold values from -0.3125 to 0.3125
- face_cross: bfloat16 [2048, 384, 384], P(('grp', 'dom')), may hold values from -0.3125 to 0.3125
- metric: float32 [2048, 384], P(('grp', 'dom')), may hold values from 0.5 to 2
- source_in: int32 [4096], P(('grp', 'dom')), may hold values from 0 to 15
- source_cross: int32 [2048], P(('grp', 'dom')), may hold values from 0 to 15
- orient_in: int32 [4096], P(('grp', 'dom')), may hold values from 0 to 7
- orient_cross: int32 [2048], P(('grp', 'dom')), may hold values from 0 to 7
- peer_in: int32 [4096, 1], P(('grp', 'dom')), may hold values from 0 to 15; in each aligned block of 32 rows (0 to 31, 32 to 63, ...) at most 3 rows name the same one
- peer_cross: int32 [2048, 1], P(('grp', 'dom')), may hold values from 0 to 7; in each aligned block of 16 rows (0 to 15, 16 to 31, ...) at most 3 rows name the same one
- target_in: int32 [4096], P(('grp', 'dom')), may hold values from 0 to 47
- target_cross: int32 [2048], P(('grp', 'dom')), may hold values from 0 to 47
Outputs:
- coarse_diag: float32 [2048, 2304], P('grp')
- coarse_face: float32 [2048, 6912], P('grp')
Inputs may be any that keep to these rules, and one draw needn't show every extreme that they name: `peer_in`: at most 3 records of one device name the same partition; on some device exactly 3 do. `peer_cross`: at most 3 records of one device name the same group; on some device exactly 3 do.
All inputs are finite; a program needn't handle non-finite values.
Results may differ from a plain program's by a relative error of at most 0.0052.
Values may be sent and summed in bfloat16 or wider, within the bound.
A program may use at most 128 MiB of HBM per device.

v0:
```python
import jax
import jax.numpy as jnp
from jax import lax
from jax.sharding import PartitionSpec as P


def corner_table(var_count):
    nodes = -1.0 + 2.0 * jnp.arange(4, dtype=jnp.float32) / 3.0
    basis = jnp.stack(((1.0 - nodes) / 2.0, (1.0 + nodes) / 2.0), axis=1)
    cube = jnp.einsum("ia,jb,kc->abcijk", basis, basis, basis).reshape(8, 64)
    return jnp.kron(jnp.eye(var_count, dtype=jnp.float32), cube)


def restrictor(weights, orient):
    var_count = weights.shape[1] // 64
    table = corner_table(var_count)
    full = weights[:, None, :] * table[None]
    shaped = full.reshape(weights.shape[0], var_count * 8, var_count, 4, 4, 4)
    bits = orient.reshape(-1, 1, 1, 1, 1, 1)
    shaped = jnp.where(bits % 2 == 1, jnp.flip(shaped, 3), shaped)
    shaped = jnp.where(bits // 2 % 2 == 1, jnp.flip(shaped, 4), shaped)
    shaped = jnp.where(bits // 4 % 2 == 1, jnp.flip(shaped, 5), shaped)
    return shaped.reshape(weights.shape[0], var_count * 8, var_count * 64).astype(jnp.bfloat16)


def pick_rows(index, table):
    picks = (index[:, None] == jnp.arange(table.shape[0], dtype=jnp.int32)[None, :]).astype(
        jnp.float32
    )
    return jnp.dot(picks, table, precision=lax.Precision.HIGHEST)


def place_rows(targets, values, row_count):
    picks = (jnp.arange(row_count, dtype=jnp.int32)[:, None] == targets[None, :]).astype(
        jnp.float32
    )
    return jnp.dot(picks, values, precision=lax.Precision.HIGHEST)


def one_sided(blocks, column_side):
    return jnp.einsum(
        "rcj,rij->rci", column_side, blocks, preferred_element_type=jnp.float32
    ).astype(jnp.bfloat16)


def coarse_terms(row_side, products):
    return jnp.einsum("rci,rdi->rcd", row_side, products, preferred_element_type=jnp.float32)


def pack_records(products, targets, peers, peer_count, capacity):
    count = products.shape[0]
    onehot = (peers[:, None] == jnp.arange(peer_count, dtype=jnp.int32)[None, :]).astype(jnp.int32)
    order_rank = jnp.sum((jnp.cumsum(onehot, axis=0) - 1) * onehot, axis=1)
    position = peers * capacity + order_rank
    places = jnp.arange(peer_count * capacity, dtype=jnp.int32)
    picks = places[:, None] == position[None, :]
    flattened = products.reshape(count, -1)
    packed = jnp.dot(
        picks.astype(jnp.bfloat16), flattened, preferred_element_type=jnp.float32
    ).astype(jnp.bfloat16)
    slot_ids = jnp.sum(jnp.where(picks, targets[None, :] + 1, 0), axis=1) - 1
    return (
        packed.reshape((peer_count, capacity) + products.shape[1:]),
        slot_ids.reshape(peer_count, capacity),
    )


def per_device(
    diag_blocks,
    face_in,
    face_cross,
    metric,
    source_in,
    source_cross,
    orient_in,
    orient_cross,
    peer_in,
    peer_cross,
    target_in,
    target_cross,
):
    elem_count = metric.shape[0]
    coarse_width = metric.shape[1] // 8
    square = coarse_width * coarse_width
    group_width = lax.axis_size("dom")
    group_count = lax.axis_size("grp")
    cross_capacity = (face_cross.shape[0] + group_count - 1) // group_count + 1
    inner_capacity = (face_in.shape[0] + group_width - 1) // group_width + 1

    def receive(packet):
        products, slot_ids = packet
        peers_here, items = slot_ids.shape
        flat_ids = slot_ids.reshape(-1)
        row_side = restrictor(
            pick_rows(flat_ids // 3, metric), jnp.zeros(flat_ids.shape, jnp.int32)
        )
        terms = coarse_terms(
            row_side, products.reshape(peers_here * items, products.shape[2], products.shape[3])
        )
        return (terms.reshape(peers_here, items, square), slot_ids)

    diag_side = restrictor(metric, jnp.zeros((elem_count,), jnp.int32))
    diag_coarse = coarse_terms(diag_side, one_sided(diag_blocks, diag_side)).reshape(
        elem_count, square
    )
    cross_side = restrictor(pick_rows(source_cross, metric), orient_cross)
    cross_products = one_sided(face_cross, cross_side)
    inner_side = restrictor(pick_rows(source_in, metric), orient_in)
    inner_products = one_sided(face_in, inner_side)
    cross_packed, cross_ids = pack_records(
        cross_products, target_cross, peer_cross[:, 0], group_count, cross_capacity
    )
    cross_terms, cross_got = receive(
        (
            lax.all_to_all(cross_packed, "grp", split_axis=0, concat_axis=0, tiled=True),
            lax.all_to_all(cross_ids, "grp", split_axis=0, concat_axis=0, tiled=True),
        )
    )
    inner_packed, inner_ids = pack_records(
        inner_products, target_in, peer_in[:, 0], group_width, inner_capacity
    )
    inner_terms, inner_got = receive(
        (
            lax.all_to_all(inner_packed, "dom", split_axis=0, concat_axis=0, tiled=True),
            lax.all_to_all(inner_ids, "dom", split_axis=0, concat_axis=0, tiled=True),
        )
    )
    face_local = place_rows(cross_got.reshape(-1), cross_terms.reshape(-1, square), 3 * elem_count)
    face_local = face_local + place_rows(
        inner_got.reshape(-1), inner_terms.reshape(-1, square), 3 * elem_count
    )
    face_local = face_local.reshape(elem_count, 3 * square)
    coarse_diag, coarse_face = (
        lax.all_gather(diag_coarse, "dom", axis=0, tiled=True),
        lax.all_gather(face_local, "dom", axis=0, tiled=True),
    )
    return (coarse_diag, coarse_face)


def solution(mesh):
    placed = (
        P(("grp", "dom"), None, None),
        P(("grp", "dom"), None, None),
        P(("grp", "dom"), None, None),
        P(("grp", "dom"), None),
        P(("grp", "dom")),
        P(("grp", "dom")),
        P(("grp", "dom")),
        P(("grp", "dom")),
        P(("grp", "dom"), None),
        P(("grp", "dom"), None),
        P(("grp", "dom")),
        P(("grp", "dom")),
    )
    return jax.shard_map(
        per_device,
        mesh=mesh,
        in_specs=placed,
        out_specs=(P("grp", None), P("grp", None)),
        check_vma=False,
    )
```

profile of v0, /device:TPU:1, one launch (start us, length us, event | category | flops | bytes accessed | tf_op | source)
XLA Modules:
  0.0 180.3 jit_solution(1263921991991287014)
XLA Ops:
  7.2 0.7 fusion.33
  7.9 0.8 select_reduce_fusion.3
  8.8 0.7 multiply_add_fusion.1
  9.4 0.1 select_reduce_fusion.2
  9.5 0.7 sub.80
  10.2 6.0 %all-to-all-start = ((s32[8,1,3]{2,1,0:T(1,128)}), s32[8,1,3]{2,1,0:T(1,128)S(1)}, u32[]{:S(2)}, u32[]{:S(2)}) async-start(s32[8,1,3]{2,1,0:T(1,128)} %bitcast.3), calls=%async_computation | async-start | bytes 8192 | tf_op jit(solution)/shard_map/all_to_all | solution.py:116
  16.2 0.1 broadcast_multiply_fusion.3
  16.3 0.1 multiply_bitcast_fusion
  16.4 0.1 mul.177
  16.5 0.1 copy.39
  16.6 0.1 mul.179
  16.7 0.1 mul.174
  16.8 0.1 mul.175
  16.9 0.1 copy.40
  17.0 4.3 %fusion.15 = f32[16,48,48]{2,1,0:T(8,128)S(1)} fusion(bf16[16,384,384]{2,1,0:T(8,128)(2,1)} %param.12, f32[48,384]{1,0:T(8,128)S(1)} %copy.40, f32[16,384]{1,0:T(8,128)} %param.15), kind=kOutput, calls=%fused_computation.25 | convolution fusion | flops 256278528 | bytes 4964352 | tf_op jit(solution)/shard_map/rci,rdi->rcd/dot_general | solution.py:47
  21.4 0.8 reshape.407
  22.3 0.4 fusion.34
  22.6 1.0 broadcast_multiply_fusion.1
  23.7 0.6 reverse_select_fusion.5
  24.3 0.7 reverse_select_fusion.4
  25.0 0.8 fusion.1
  25.8 0.1 slice-done.1
  25.9 1.8 fusion.12
  27.6 0.9 copy.51
  28.6 0.4 fusion.26
  29.0 1.9 %broadcast_multiply_fusion = bf16[32,48,6,4,4,4]{1,0,5,4,3,2:T(8,128)(2,1)S(1)} fusion(f32[48,6,4,4,4]{0,4,3,2,1:T(4,128)S(1)} %broadcast_multiply_fusion.2, f32[32,6,4,4,4]{0,4,3,2,1:T(4,128)S(1)} %bitcast.55), kind=kLoop, calls=%fused_computation.14 | loop fusion | flops 1179648 | bytes 1302528 | tf_op jit(solution)/shard_map/mul | solution.py:17
  31.0 0.1 fusion.25
  31.1 0.1 reduce_window_sum.23
  31.1 0.2 select_reduce_fusion.1
  31.3 1.0 reverse_select_fusion.2
  32.4 0.1 select_reduce_fusion
  32.5 1.5 reverse_select_fusion.1
  34.0 1.1 fusion
  35.1 0.7 sub.86
  35.8 7.6 %all-to-all-start.2 = ((s32[16,1,3]{2,1,0:T(1,128)}), s32[16,1,3]{2,1,0:T(1,128)S(1)}, u32[]{:S(2)}, u32[]{:S(2)}) async-start(s32[16,1,3]{2,1,0:T(1,128)} %bitcast.8), calls=%async_computation.2 | async-start | bytes 16384 | tf_op jit(solution)/shard_map/all_to_all | solution.py:125
  43.4 1.6 convolution_convert_fusion.1
  45.0 1.0 copy.52
  46.0 3.8 %all-to-all-done.2 = s32[16,1,3]{2,1,0:T(1,128)S(1)} async-done(((s32[16,1,3]{2,1,0:T(1,128)}), s32[16,1,3]{2,1,0:T(1,128)S(1)}, u32[]{:S(2)}, u32[]{:S(2)}) %all-to-all-start.2) | async-done | bytes 224 | tf_op jit(solution)/shard_map/all_to_all | solution.py:125
  49.9 6.1 %all-to-all-start.1 = ((bf16[8,3,48,384]{3,2,1,0:T(8,128)(2,1)}), bf16[8,3,48,384]{3,2,1,0:T(8,128)(2,1)}, u32[]{:S(2)}, u32[]{:S(2)}) async-start(bf16[8,3,48,384]{3,2,1,0:T(8,128)(2,1)} %bitcast.49), calls=%async_computation.1 | async-start | bytes 1769472 | tf_op jit(solution)/shard_map/all_to_all | solution.py:115
  55.9 7.7 %fusion.9 = bf16[32,48,384]{2,1,0:T(8,128)(2,1)S(1)} fusion(bf16[32,384,384]{2,1,0:T(8,128)(2,1)} %param.13, bf16[32,48,384]{1,0,2:T(8,128)(2,1)S(1)} %bitcast.42), kind=kOutput, calls=%fused_computation.22 | convolution fusion | flops 453574656 | bytes 11796480 | tf_op jit(solution)/shard_map/rcj,rij->rci/dot_general | solution.py:41
  63.7 0.3 copy.53
  63.9 0.7 convolution_convert_fusion
  64.7 1.4 copy.54
  66.1 3.1 %all-to-all-done.1 = bf16[8,3,48,384]{3,2,1,0:T(8,128)(2,1)} async-done(((bf16[8,3,48,384]{3,2,1,0:T(8,128)(2,1)}), bf16[8,3,48,384]{3,2,1,0:T(8,128)(2,1)}, u32[]{:S(2)}, u32[]{:S(2)}) %all-to-all-start.1) | async-done | bytes 884768 | tf_op jit(solution)/shard_map/all_to_all | solution.py:115
  69.3 3.7 %all-to-all-start.3 = ((bf16[16,3,48,384]{3,2,1,0:T(8,128)(2,1)}), bf16[16,3,48,384]{3,2,1,0:T(8,128)(2,1)S(1)}, u32[]{:S(2)}, u32[]{:S(2)}) async-start(bf16[16,3,48,384]{3,2,1,0:T(8,128)(2,1)} %bitcast.23), calls=%async_computation.3 | async-start | bytes 3538944 | tf_op jit(solution)/shard_map/all_to_all | solution.py:124
  73.0 0.0 all-gather.5.cloned.1.call-start
  73.0 0.5 broadcast.910
  73.5 0.7 reduce.6
  74.2 0.1 eq.232
  74.3 0.2 fusion.30
  74.5 0.7 reduce.7
  75.2 0.1 eq.251
  75.3 0.2 fusion.24
  75.5 1.6 fusion.16
  77.1 0.3 reshape_reshape.6
  77.4 0.3 fusion.23
  77.7 21.1 %all-to-all-done.3 = bf16[16,3,48,384]{3,2,1,0:T(8,128)(2,1)S(1)} async-done(((bf16[16,3,48,384]{3,2,1,0:T(8,128)(2,1)}), bf16[16,3,48,384]{3,2,1,0:T(8,128)(2,1)S(1)}, u32[]{:S(2)}, u32[]{:S(2)}) %all-to-all-start.3) | async-done | bytes 1769504 | tf_op jit(solution)/shard_map/all_to_all | solution.py:124
  98.9 0.7 fusion.4
  99.6 0.5 reshape_reshape.7
  100.2 0.3 convolution_add_fusion
  100.5 0.9 reshape.414
  101.4 62.3 %all-gather.5.cloned.1.call-done = f32[256,6912]{1,0:T(8,128)} async-done(((f32[16,6912]{1,0:T(8,128)}), f32[256,6912]{1,0:T(8,128)}) %all-gather.5.cloned.1.call-update) | async-done | bytes 7077904 | tf_op jit(solution)/shard_map/all_gather | solution.py:135
  163.8 3.2 %copy.65 = f32[256,2304]{1,0:T(8,128)} copy(f32[256,2304]{1,0:T(8,128)} %all-gather.3.cloned.1.call-done) | data formatting | bytes 4718592
  167.0 6.4 %copy.66 = f32[256,6912]{1,0:T(8,128)} copy(f32[256,6912]{1,0:T(8,128)} %all-gather.5.cloned.1.call-done) | data formatting | bytes 14155776
  (36 shorter events, 0.3 us)
Async XLA Ops:
  10.2 25.6 %all-to-all-start = ((s32[8,1,3]{2,1,0:T(1,128)}), s32[8,1,3]{2,1,0:T(1,128)S(1)}, u32[]{:S(2)}, u32[]{:S(2)}) async-start(s32[8,1,3]{2,1,0:T(1,128)} %bitcast.3), calls=%async_computation | async-start | bytes 8192 | tf_op jit(solution)/shard_map/all_to_all | solution.py:116
  16.2 85.3 %all-gather.3.cloned.1.call-start = ((), (), s32[]{:S(2)}) async-start(), calls=%async_computation.4 | async-start | bytes 2506752 | tf_op jit(solution)/shard_map/all_gather | solution.py:134
  17.0 5.2 %copy-start = (f32[16,384]{1,0:T(8,128)S(1)}, f32[16,384]{1,0:T(8,128)}, u32[]{:S(2)}) copy-start(f32[16,384]{1,0:T(8,128)} %param.15) | copy-start | bytes 73732
  17.0 5.2 %copy-start.2 = (s32[16]{0:T(128)S(1)}, s32[16]{0:T(128)}, u32[]{:S(2)}) copy-start(s32[16]{0:T(128)} %param.17) | copy-start | bytes 196
  17.0 8.7 %slice-start = ((s8[4718592]{0:T(1024)(128)(4,1)}), s8[524288]{0:T(1024)(128)(4,1)S(1)}, s32[]{:S(2)}) async-start(s8[4718592]{0:T(1024)(128)(4,1)} %bitcast.46), calls=%async_computation.6 | async-start | bytes 1048576
  21.4 2.3 %copy-start.5 = (s32[16]{0:T(128)S(1)}, s32[16]{0:T(128)}, u32[]{:S(2)}) copy-start(s32[16]{0:T(128)} %param.19) | copy-start | bytes 196
  23.7 2.2 %slice-start.1 = ((s8[4718592]{0:T(1024)(128)(4,1)}), s8[4194304]{0:T(1024)(128)(4,1)S(1)}, s32[]{:S(2)}) async-start(s8[4718592]{0:T(1024)(128)(4,1)} %bitcast.46), calls=%async_computation.7 | async-start | bytes 8388608
  25.9 2.7 %copy-start.3 = (s32[32]{0:T(128)S(1)}, s32[32]{0:T(128)}, u32[]{:S(2)}) copy-start(s32[32]{0:T(128)} %param.16) | copy-start | bytes 388
  29.0 2.0 %copy-start.6 = (s32[32]{0:T(128)S(1)}, s32[32]{0:T(128)}, u32[]{:S(2)}) copy-start(s32[32]{0:T(128)} %param.18) | copy-start | bytes 388
  29.0 2.0 %copy-start.1 = (s32[32,1]{0,1:T(1,128)S(1)}, s32[32,1]{0,1:T(1,128)}, u32[]{:S(2)}) copy-start(s32[32,1]{0,1:T(1,128)} %param.20) | copy-start | bytes 388
  31.3 1.1 copy-start.4
  35.8 14.0 %all-to-all-start.2 = ((s32[16,1,3]{2,1,0:T(1,128)}), s32[16,1,3]{2,1,0:T(1,128)S(1)}, u32[]{:S(2)}, u32[]{:S(2)}) async-start(s32[16,1,3]{2,1,0:T(1,128)} %bitcast.8), calls=%async_computation.2 | async-start | bytes 16384 | tf_op jit(solution)/shard_map/all_to_all | solution.py:125
  49.9 19.4 %all-to-all-start.1 = ((bf16[8,3,48,384]{3,2,1,0:T(8,128)(2,1)}), bf16[8,3,48,384]{3,2,1,0:T(8,128)(2,1)}, u32[]{:S(2)}, u32[]{:S(2)}) async-start(bf16[8,3,48,384]{3,2,1,0:T(8,128)(2,1)} %bitcast.49), calls=%async_computation.1 | async-start | bytes 1769472 | tf_op jit(solution)/shard_map/all_to_all | solution.py:115
  69.3 29.6 %all-to-all-start.3 = ((bf16[16,3,48,384]{3,2,1,0:T(8,128)(2,1)}), bf16[16,3,48,384]{3,2,1,0:T(8,128)(2,1)S(1)}, u32[]{:S(2)}, u32[]{:S(2)}) async-start(bf16[16,3,48,384]{3,2,1,0:T(8,128)(2,1)} %bitcast.23), calls=%async_computation.3 | async-start | bytes 3538944 | tf_op jit(solution)/shard_map/all_to_all | solution.py:124
  73.0 90.8 %all-gather.5.cloned.1.call-start = ((), (), s32[]{:S(2)}) async-start(), calls=%async_computation.5 | async-start | bytes 7520256 | tf_op jit(solution)/shard_map/all_gather | solution.py:135
Sparse Core Ops, SparseCore 0:
  22.4 46.2 all-gather.2
  101.5 62.1 all-gather.4
where the time goes:
time: 181 us; the launch traced here: 180 us
  waiting for transfers between devices  90.5 us (50%)
  starting transfers between devices  23.4 us (13%)
  matrix products  20.3 us (11%)
  local copies, waits for them, and re-layouts  18.6 us (10%)
  between operations  14.4 us (8%)
  other arithmetic  13.1 us (7%)
    all_gather x1, waiting for transfers between devices, per_device(): lax.all_gather(face_local, 'dom', axis=0, tiled=True)  62.3 us
    all_to_all x1, waiting for transfers between devices, per_device(): lax.all_to_all(inner_packed, 'dom', split_axis=0, concat_axis=0, tiled=True)  21.1 us
    unnamed x24, local copies, waits for them, and re-layouts  13.4 us
    dot_general x2, matrix products, one_sided(): jnp.einsum('rcj,rij->rci', column_side, blocks, preferred_element_type=jn...  9.53 us
    all_to_all x1, starting transfers between devices, per_device(): lax.all_to_all(inner_ids, 'dom', split_axis=0, concat_axis=0, tiled=True)  7.6 us
    dot_general x3, matrix products, coarse_terms(): jnp.einsum('rci,rdi->rcd', row_side, products, preferred_element_type=jnp...  6.65 us
    all_to_all x1, starting transfers between devices, per_device(): lax.all_to_all(cross_packed, 'grp', split_axis=0, concat_axis=0, tiled=True)  6.07 us
    all_to_all x1, starting transfers between devices, per_device(): lax.all_to_all(cross_ids, 'grp', split_axis=0, concat_axis=0, tiled=True)  5.96 us
  transfers between devices with their start and end apart: 6, of which 4 were waited for; matrix products, arithmetic and copies ran while one was open for 22% of the time, Pallas kernels for 0%

commit v1 on v0

--- a/solution.py
+++ b/solution.py
@@ -2,6 +2,29 @@
 import jax.numpy as jnp
 from jax import lax
 from jax.sharding import PartitionSpec as P
+
+
+def cut_along(x, dim, count):
+    shape = x.shape
+    blocks = x.reshape(*shape[:dim], count, shape[dim] // count, *shape[dim + 1 :])
+    return jnp.moveaxis(blocks, dim, 0)
+
+
+def in_order(blocks, dim):
+    shape = list(blocks.shape[1:])
+    shape[dim] *= blocks.shape[0]
+    return jnp.moveaxis(blocks, 0, dim).reshape(shape)
+
+
+def swapped_with_each(x, axis, split_dim, concat_dim):
+    count, here = (lax.axis_size(axis), lax.axis_index(axis))
+    blocks = cut_along(x, split_dim, count)
+    outs = [blocks[here]]
+    for step in range(1, count):
+        sent = blocks[here ^ step]
+        outs.append(lax.ppermute(sent, axis, [(i, i ^ step) for i in range(count)]))
+    blocks = jnp.stack(outs)[here ^ jnp.arange(count)]
+    return in_order(blocks, concat_dim)
 
 
 def corner_table(var_count):
@@ -113,7 +136,7 @@
     cross_terms, cross_got = receive(
         (
             lax.all_to_all(cross_packed, "grp", split_axis=0, concat_axis=0, tiled=True),
-            lax.all_to_all(cross_ids, "grp", split_axis=0, concat_axis=0, tiled=True),
+            swapped_with_each(cross_ids, "grp", 0, 0),
         )
     )
     inner_packed, inner_ids = pack_records(

time: 181 us -> 179 us (0.989)
  waiting for transfers between devices: 90.5 us -> 79.9 us
  starting transfers between devices: 23.4 us -> 30.2 us
  local copies, waits for them, and re-layouts: 18.6 us -> 20.8 us
    all_to_all x1, waiting for transfers between devices: 21.1 us -> 8.92 us  [per_device(): lax.all_to_all(inner_packed, 'dom', split_axis=0, concat_axis=0, tiled=True)]
    ppermute x0 -> x7, starting transfers between devices: none -> 9.34 us  [swapped_with_each(): outs.append(lax.ppermute(sent, axis, [(i, i ^ step) for i in range(count)]))]
    all_to_all x1 -> x0, starting transfers between devices: 5.96 us -> none  [per_device(): lax.all_to_all(cross_ids, 'grp', split_axis=0, concat_axis=0, tiled=True)]
    all_to_all x1, waiting for transfers between devices: 3.84 us -> 0.01 us  [per_device(): lax.all_to_all(inner_ids, 'dom', split_axis=0, concat_axis=0, tiled=True)]
    all_gather x1, waiting for transfers between devices: 62.3 us -> 65.8 us  [per_device(): lax.all_gather(face_local, 'dom', axis=0, tiled=True)]
    all_to_all x1, starting transfers between devices: 3.71 us -> 6.93 us  [per_device(): lax.all_to_all(inner_packed, 'dom', split_axis=0, concat_axis=0, tiled=True)]
    ppermute x0 -> x7, waiting for transfers between devices: none -> 1.99 us  [swapped_with_each(): outs.append(lax.ppermute(sent, axis, [(i, i ^ step) for i in range(count)]))]
  transfers between devices with their start and end apart: 6 -> 12, of which waited for: 4 -> 5; matrix products, arithmetic and copies ran while one was open for 22% -> 23% of each run, Pallas kernels for 0% -> 0%
where the time goes in v1:
time: 179 us
  waiting for transfers between devices  79.9 us (45%)
  starting transfers between devices  30.2 us (17%)
  matrix products  21 us (12%)
  local copies, waits for them, and re-layouts  20.8 us (12%)
  between operations  14.5 us (8%)
  other arithmetic  12.2 us (7%)
    all_gather x1, waiting for transfers between devices, per_device(): lax.all_gather(face_local, 'dom', axis=0, tiled=True)  65.8 us
    unnamed x24, local copies, waits for them, and re-layouts  14.8 us
    dot_general x2, matrix products, one_sided(): jnp.einsum('rcj,rij->rci', column_side, blocks, preferred_element_type=jn...  10.4 us
    ppermute x7, starting transfers between devices, swapped_with_each(): outs.append(lax.ppermute(sent, axis, [(i, i ^ step) for i in range(count)]))  9.34 us
    all_to_all x1, waiting for transfers between devices, per_device(): lax.all_to_all(inner_packed, 'dom', split_axis=0, concat_axis=0, tiled=True)  8.92 us
    all_to_all x1, starting transfers between devices, per_device(): lax.all_to_all(inner_ids, 'dom', split_axis=0, concat_axis=0, tiled=True)  8.42 us
    all_to_all x1, starting transfers between devices, per_device(): lax.all_to_all(inner_packed, 'dom', split_axis=0, concat_axis=0, tiled=True)  6.93 us
    dot_general x3, matrix products, coarse_terms(): jnp.einsum('rci,rdi->rcd', row_side, products, preferred_element_type=jnp...  6.62 us
  transfers between devices with their start and end apart: 12, of which 5 were waited for; matrix products, arithmetic and copies ran while one was open for 23% of the time, Pallas kernels for 0%

profile of v1, /device:TPU:1, one launch (start us, length us, event | category | flops | bytes accessed | tf_op | source)
XLA Modules:
  0.0 178.6 jit_solution(18259577969441913857)
XLA Ops:
  7.2 0.7 fusion.25
  7.9 0.8 select_reduce_fusion.1
  8.8 0.7 multiply_add_fusion
  9.5 0.1 select_reduce_fusion
  9.6 0.7 sub.86
  10.2 8.4 %all-to-all-start.1 = ((s32[16,1,3]{2,1,0:T(1,128)}), s32[16,1,3]{2,1,0:T(1,128)S(1)}, u32[]{:S(2)}, u32[]{:S(2)}) async-start(s32[16,1,3]{2,1,0:T(1,128)} %bitcast.23), calls=%async_computation.1 | async-start | bytes 16384 | tf_op jit(solution)/shard_map/all_to_all | solution.py:148
  18.9 0.1 mul.177
  19.2 0.1 mul.179
  19.5 0.1 copy.75
  19.6 4.3 %fusion.15 = f32[16,48,48]{2,1,0:T(8,128)S(1)} fusion(bf16[16,384,384]{2,1,0:T(8,128)(2,1)} %param.12, f32[48,384]{1,0:T(8,128)S(1)} %copy.75, f32[16,384]{1,0:T(8,128)} %param.15), kind=kOutput, calls=%fused_computation.26 | convolution fusion | flops 256278528 | bytes 4964352 | tf_op jit(solution)/shard_map/rci,rdi->rcd/dot_general | solution.py:70
  23.9 0.8 reshape.416
  24.9 0.2 select_reduce_fusion.3
  25.1 0.4 fusion.34
  25.5 1.0 broadcast_multiply_fusion.1
  26.5 0.4 fusion.26
  26.9 1.9 %broadcast_multiply_fusion = bf16[32,48,6,4,4,4]{1,0,5,4,3,2:T(8,128)(2,1)S(1)} fusion(f32[48,6,4,4,4]{0,4,3,2,1:T(4,128)S(1)} %broadcast_multiply_fusion.2, f32[32,6,4,4,4]{0,4,3,2,1:T(4,128)S(1)} %bitcast.78), kind=kLoop, calls=%fused_computation.15 | loop fusion | flops 1179648 | bytes 1302528 | tf_op jit(solution)/shard_map/mul | solution.py:40
  29.0 0.6 reverse_select_fusion.5
  29.6 0.7 reverse_select_fusion.4
  30.4 0.8 fusion.1
  31.1 2.6 %fusion.12 = bf16[16,48,384]{2,1,0:T(8,128)(2,1)} fusion(bf16[16,384,384]{2,1,0:T(8,128)(2,1)S(1)} %bitcast.70, bf16[16,48,384]{1,0,2:T(8,128)(2,1)S(1)} %bitcast.67), kind=kOutput, calls=%fused_computation.24 | convolution fusion | flops 226787328 | bytes 5898240 | tf_op jit(solution)/shard_map/rcj,rij->rci/dot_general | solution.py:64
  33.8 1.0 reverse_select_fusion.2
  34.8 1.2 copy.95
  36.0 1.4 convolution_convert_fusion.1
  37.4 1.3 reverse_select_fusion.1
  38.7 1.1 fusion
  39.9 2.2 %copy.96 = bf16[3,8,48,384]{3,2,1,0:T(8,128)(2,1)} copy(bf16[3,8,48,384]{3,1,2,0:T(8,128)(2,1)} %bitcast.73) | data formatting | bytes 1769472
  42.1 5.4 %all-to-all-start = ((bf16[8,3,48,384]{3,2,1,0:T(8,128)(2,1)}), bf16[8,3,48,384]{3,2,1,0:T(8,128)(2,1)}, u32[]{:S(2)}, u32[]{:S(2)}) async-start(bf16[8,3,48,384]{3,2,1,0:T(8,128)(2,1)} %bitcast.72), calls=%async_computation | async-start | bytes 1769472 | tf_op jit(solution)/shard_map/all_to_all | solution.py:138
  47.6 7.7 %fusion.9 = bf16[32,48,384]{2,1,0:T(8,128)(2,1)S(1)} fusion(bf16[32,384,384]{2,1,0:T(8,128)(2,1)} %param.13, bf16[32,48,384]{1,0,2:T(8,128)(2,1)S(1)} %bitcast.65), kind=kOutput, calls=%fused_computation.23 | convolution fusion | flops 453574656 | bytes 11796480 | tf_op jit(solution)/shard_map/rcj,rij->rci/dot_general | solution.py:64
  55.3 0.3 copy.97
  55.6 0.7 convolution_convert_fusion
  56.3 1.4 copy.98
  57.7 3.1 %all-to-all-done = bf16[8,3,48,384]{3,2,1,0:T(8,128)(2,1)} async-done(((bf16[8,3,48,384]{3,2,1,0:T(8,128)(2,1)}), bf16[8,3,48,384]{3,2,1,0:T(8,128)(2,1)}, u32[]{:S(2)}, u32[]{:S(2)}) %all-to-all-start) | async-done | bytes 884768 | tf_op jit(solution)/shard_map/all_to_all | solution.py:138
  60.9 6.9 %all-to-all-start.2 = ((bf16[16,3,48,384]{3,2,1,0:T(8,128)(2,1)}), bf16[16,3,48,384]{3,2,1,0:T(8,128)(2,1)S(1)}, u32[]{:S(2)}, u32[]{:S(2)}) async-start(bf16[16,3,48,384]{3,2,1,0:T(8,128)(2,1)} %bitcast.38), calls=%async_computation.2 | async-start | bytes 3538944 | tf_op jit(solution)/shard_map/all_to_all | solution.py:147
  67.9 1.3 collective-permute-start
  69.2 0.3 collective-permute-start.1
  69.5 1.4 collective-permute-start.2
  71.0 0.4 collective-permute-start.3
  71.4 2.9 %collective-permute-start.4 = (s32[1,3]{1,0:T(1,128)S(1)}, s32[1,3]{1,0:T(1,128)S(1)}, u32[]{:S(2)}, u32[]{:S(2)}) collective-permute-start(s32[1,3]{1,0:T(1,128)S(1)} %get-tuple-element.4), channel_id=1, source_target_pairs={{0,80},{16,64},{32,112},{48,96},{64,16},{80,0},{96,48},{112,32},{1... | collective-permute-start | bytes 44 | tf_op jit(solution)/shard_map/ppermute | solution.py:25
  74.2 0.1 copy.76
  74.3 1.0 collective-permute-start.5
  75.3 0.1 copy.77
  75.4 2.0 %collective-permute-start.6 = (s32[1,3]{1,0:T(1,128)S(1)}, s32[1,3]{1,0:T(1,128)S(1)}, u32[]{:S(2)}, u32[]{:S(2)}) collective-permute-start(s32[1,3]{1,0:T(1,128)S(1)} %get-tuple-element.2), channel_id=1, source_target_pairs={{0,112},{16,96},{32,80},{48,64},{64,48},{80,32},{96,16},{112,0},{1... | collective-permute-start | bytes 44 | tf_op jit(solution)/shard_map/ppermute | solution.py:25
  77.5 0.1 copy.78
  77.5 0.1 copy.79
  77.8 0.6 collective-permute-done.5
  78.4 0.1 copy.82
  78.5 1.4 collective-permute-done.6
  80.0 0.1 stack.49
  80.2 0.6 gather_fusion
  80.9 0.2 fusion.30
  81.1 0.5 broadcast.941
  81.6 0.7 reduce.3
  82.4 0.2 fusion.24
  82.6 1.6 fusion.16
  84.2 0.3 reshape_reshape.8
  84.5 0.3 fusion.23
  84.8 8.9 %all-to-all-done.2 = bf16[16,3,48,384]{3,2,1,0:T(8,128)(2,1)S(1)} async-done(((bf16[16,3,48,384]{3,2,1,0:T(8,128)(2,1)}), bf16[16,3,48,384]{3,2,1,0:T(8,128)(2,1)S(1)}, u32[]{:S(2)}, u32[]{:S(2)}) %all-to-all-start.2) | async-done | bytes 1769504 | tf_op jit(solution)/shard_map/all_to_all | solution.py:147
  93.7 0.7 fusion.4
  94.5 0.5 reshape_reshape.9
  95.0 0.3 convolution_add_fusion
  95.4 0.9 reshape.423
  96.3 65.8 %all-gather.5.cloned.1.call-done = f32[256,6912]{1,0:T(8,128)} async-done(((f32[16,6912]{1,0:T(8,128)}), f32[256,6912]{1,0:T(8,128)}) %all-gather.5.cloned.1.call-update) | async-done | bytes 7077904 | tf_op jit(solution)/shard_map/all_gather | solution.py:158
  162.1 3.2 %copy.109 = f32[256,2304]{1,0:T(8,128)} copy(f32[256,2304]{1,0:T(8,128)} %all-gather.3.cloned.1.call-done) | data formatting | bytes 4718592
  165.3 6.4 %copy.110 = f32[256,6912]{1,0:T(8,128)} copy(f32[256,6912]{1,0:T(8,128)} %all-gather.5.cloned.1.call-done) | data formatting | bytes 14155776
  (61 shorter events, 1.7 us)
Async XLA Ops:
  10.2 31.9 %all-to-all-start.1 = ((s32[16,1,3]{2,1,0:T(1,128)}), s32[16,1,3]{2,1,0:T(1,128)S(1)}, u32[]{:S(2)}, u32[]{:S(2)}) async-start(s32[16,1,3]{2,1,0:T(1,128)} %bitcast.23), calls=%async_computation.1 | async-start | bytes 16384 | tf_op jit(solution)/shard_map/all_to_all | solution.py:148
  18.7 77.6 %all-gather.3.cloned.1.call-start = ((), (), s32[]{:S(2)}) async-start(), calls=%async_computation.3 | async-start | bytes 2506752 | tf_op jit(solution)/shard_map/all_gather | solution.py:157
  19.6 5.2 %copy-start.1 = (s32[16,1]{0,1:T(1,128)S(1)}, s32[16,1]{0,1:T(1,128)}, u32[]{:S(2)}) copy-start(s32[16,1]{0,1:T(1,128)} %param.21) | copy-start | bytes 196
  19.6 5.5 %copy-start = (f32[16,384]{1,0:T(8,128)S(1)}, f32[16,384]{1,0:T(8,128)}, u32[]{:S(2)}) copy-start(f32[16,384]{1,0:T(8,128)} %param.15) | copy-start | bytes 73732
  19.6 5.5 %copy-start.2 = (s32[16]{0:T(128)S(1)}, s32[16]{0:T(128)}, u32[]{:S(2)}) copy-start(s32[16]{0:T(128)} %param.17) | copy-start | bytes 196
  23.9 2.6 %copy-start.5 = (s32[16]{0:T(128)S(1)}, s32[16]{0:T(128)}, u32[]{:S(2)}) copy-start(s32[16]{0:T(128)} %param.19) | copy-start | bytes 196
  23.9 2.6 %copy-start.3 = (s32[32]{0:T(128)S(1)}, s32[32]{0:T(128)}, u32[]{:S(2)}) copy-start(s32[32]{0:T(128)} %param.16) | copy-start | bytes 388
  26.5 2.4 %copy-start.6 = (s32[32]{0:T(128)S(1)}, s32[32]{0:T(128)}, u32[]{:S(2)}) copy-start(s32[32]{0:T(128)} %param.18) | copy-start | bytes 388
  26.5 2.4 %copy-start.4 = (s32[16]{0:T(128)S(1)}, s32[16]{0:T(128)}, u32[]{:S(2)}) copy-start(s32[16]{0:T(128)} %param.23) | copy-start | bytes 196
  26.9 4.2 %slice-start = ((s8[4718592]{0:T(1024)(128)(4,1)}), s8[4194304]{0:T(1024)(128)(4,1)S(1)}, s32[]{:S(2)}) async-start(s8[4718592]{0:T(1024)(128)(4,1)} %bitcast.69), calls=%async_computation.5 | async-start | bytes 8388608
  29.0 2.1 %slice-start.1 = ((s8[4718592]{0:T(1024)(128)(4,1)}), s8[524288]{0:T(1024)(128)(4,1)S(1)}, s32[]{:S(2)}) async-start(s8[4718592]{0:T(1024)(128)(4,1)} %bitcast.69), calls=%async_computation.6 | async-start | bytes 1048576
  42.1 18.8 %all-to-all-start = ((bf16[8,3,48,384]{3,2,1,0:T(8,128)(2,1)}), bf16[8,3,48,384]{3,2,1,0:T(8,128)(2,1)}, u32[]{:S(2)}, u32[]{:S(2)}) async-start(bf16[8,3,48,384]{3,2,1,0:T(8,128)(2,1)} %bitcast.72), calls=%async_computation | async-start | bytes 1769472 | tf_op jit(solution)/shard_map/all_to_all | solution.py:138
  60.9 32.9 %all-to-all-start.2 = ((bf16[16,3,48,384]{3,2,1,0:T(8,128)(2,1)}), bf16[16,3,48,384]{3,2,1,0:T(8,128)(2,1)S(1)}, u32[]{:S(2)}, u32[]{:S(2)}) async-start(bf16[16,3,48,384]{3,2,1,0:T(8,128)(2,1)} %bitcast.38), calls=%async_computation.2 | async-start | bytes 3538944 | tf_op jit(solution)/shard_map/all_to_all | solution.py:147
  67.8 94.3 %all-gather.5.cloned.1.call-start = ((), (), s32[]{:S(2)}) async-start(), calls=%async_computation.4 | async-start | bytes 7520256 | tf_op jit(solution)/shard_map/all_gather | solution.py:158
  67.9 6.4 %collective-permute-start = (s32[1,3]{1,0:T(1,128)S(1)}, s32[1,3]{1,0:T(1,128)S(1)}, u32[]{:S(2)}, u32[]{:S(2)}) collective-permute-start(s32[1,3]{1,0:T(1,128)S(1)} %get-tuple-element.8), channel_id=1, source_target_pairs={{0,16},{16,0},{32,48},{48,32},{64,80},{80,64},{96,112},{112,96},{1... | collective-permute-start | bytes 44 | tf_op jit(solution)/shard_map/ppermute | solution.py:25
  69.2 6.2 %collective-permute-start.1 = (s32[1,3]{1,0:T(1,128)S(1)}, s32[1,3]{1,0:T(1,128)S(1)}, u32[]{:S(2)}, u32[]{:S(2)}) collective-permute-start(s32[1,3]{1,0:T(1,128)S(1)} %get-tuple-element.7), channel_id=1, source_target_pairs={{0,32},{16,48},{32,0},{48,16},{64,96},{80,112},{96,64},{112,80},{1... | collective-permute-start | bytes 44 | tf_op jit(solution)/shard_map/ppermute | solution.py:25
  69.5 8.0 %collective-permute-start.2 = (s32[1,3]{1,0:T(1,128)S(1)}, s32[1,3]{1,0:T(1,128)S(1)}, u32[]{:S(2)}, u32[]{:S(2)}) collective-permute-start(s32[1,3]{1,0:T(1,128)S(1)} %get-tuple-element.6), channel_id=1, source_target_pairs={{0,48},{16,32},{32,16},{48,0},{64,112},{80,96},{96,80},{112,64},{1... | collective-permute-start | bytes 44 | tf_op jit(solution)/shard_map/ppermute | solution.py:25
  71.0 6.7 %collective-permute-start.3 = (s32[1,3]{1,0:T(1,128)S(1)}, s32[1,3]{1,0:T(1,128)S(1)}, u32[]{:S(2)}, u32[]{:S(2)}) collective-permute-start(s32[1,3]{1,0:T(1,128)S(1)} %get-tuple-element.5), channel_id=1, source_target_pairs={{0,64},{16,80},{32,96},{48,112},{64,0},{80,16},{96,32},{112,48},{1... | collective-permute-start | bytes 44 | tf_op jit(solution)/shard_map/ppermute | solution.py:25
  71.4 6.4 %collective-permute-start.4 = (s32[1,3]{1,0:T(1,128)S(1)}, s32[1,3]{1,0:T(1,128)S(1)}, u32[]{:S(2)}, u32[]{:S(2)}) collective-permute-start(s32[1,3]{1,0:T(1,128)S(1)} %get-tuple-element.4), channel_id=1, source_target_pairs={{0,80},{16,64},{32,112},{48,96},{64,16},{80,0},{96,48},{112,32},{1... | collective-permute-start | bytes 44 | tf_op jit(solution)/shard_map/ppermute | solution.py:25
  74.3 4.1 %collective-permute-start.5 = (s32[1,3]{1,0:T(1,128)S(1)}, s32[1,3]{1,0:T(1,128)S(1)}, u32[]{:S(2)}, u32[]{:S(2)}) collective-permute-start(s32[1,3]{1,0:T(1,128)S(1)} %get-tuple-element.3), channel_id=1, source_target_pairs={{0,96},{16,112},{32,64},{48,80},{64,32},{80,48},{96,0},{112,16},{1... | collective-permute-start | bytes 44 | tf_op jit(solution)/shard_map/ppermute | solution.py:25
  75.4 4.5 %collective-permute-start.6 = (s32[1,3]{1,0:T(1,128)S(1)}, s32[1,3]{1,0:T(1,128)S(1)}, u32[]{:S(2)}, u32[]{:S(2)}) collective-permute-start(s32[1,3]{1,0:T(1,128)S(1)} %get-tuple-element.2), channel_id=1, source_target_pairs={{0,112},{16,96},{32,80},{48,64},{64,48},{80,32},{96,16},{112,0},{1... | collective-permute-start | bytes 44 | tf_op jit(solution)/shard_map/ppermute | solution.py:25
Sparse Core Ops, SparseCore 0:
  24.9 46.2 all-gather.2
  96.4 65.6 all-gather.4
